TPU v7x, 32 devices: a whole 2x2x4 slice. The times are simulated.
32 devices in a mesh: row: 8 (over y, x, core), col: 4 (over z).
Axes of the slice: x: 2, y: 2, z: 4, core: 2. Of those that a mesh axis runs over, the one named last changes fastest.
Arguments:
- documents: float32 [6144, 768], P('row', 'col'), may hold values from -6 to 6
- projection: float32 [768, 768], P('col'), may hold values from -0.21875 to 0.21875
- landmarks: float32 [16384, 768], P('col', 'row'), may hold values from -6 to 6
- coefficients: float32 [16384, 128], P('col'), may hold values from -6 to 6
- inverse_tiles: float32 [16384, 16384], P('col', 'row'), may hold values from -0.046875 to 0.046875
- labels: int32 [6144, 128], P('row'), may hold values 0 or 1
Outputs:
- new_coefficients: float32 [16384, 128], P('col')
- residual: float32 [6144, 128], P('row')
All inputs are finite; a program needn't handle non-finite values. No bound on the sum of `labels` on one device may be relied on, other than what follows from the above.
Results may differ from a plain program's by a relative error of at most 0.0001.
Values sent between devices are 32-bit elements; how exact they have to be, the bound alone decides.
A program may use at most 128 MiB of HBM per device.

v0:
```python
import jax
import jax.numpy as jnp
from jax import lax
from jax.sharding import PartitionSpec as P

ITERS = 2


def broadcast(block, axis, owner):
    block = jnp.where(lax.axis_index(axis) == owner, block, jnp.zeros_like(block))
    return lax.psum(block, axis)


def on_device(documents, projection, landmarks, coefficients, inverse_tiles, labels):
    highest = lax.Precision.HIGHEST
    land_full = lax.all_gather(landmarks, "row", axis=1, tiled=True)
    sq_land = jnp.sum(land_full * land_full, axis=1)
    feature_width = land_full.shape[1]
    proj_share = lax.psum_scatter(
        jnp.dot(documents, projection, precision=highest, preferred_element_type=jnp.float32),
        "col",
        scatter_dimension=0,
        tiled=True,
    )
    rows_in = lax.all_gather(proj_share, "col", axis=0, tiled=True)
    sq_doc = jnp.sum(rows_in * rows_in, axis=1)
    inner = lax.dot_general(
        rows_in,
        land_full,
        (((1,), (1,)), ((), ())),
        precision=highest,
        preferred_element_type=jnp.float32,
    )
    kernel = jnp.exp(-2.0 * (sq_doc[:, None] + sq_land[None, :] - 2.0 * inner) / feature_width)
    row_count = lax.axis_size("row")
    col_count = lax.axis_size("col")
    step_size = 64.0 / (documents.shape[0] * row_count)
    block_rows = inverse_tiles.shape[1]
    group_size = row_count // col_count
    row_index = lax.axis_index("row")
    source = row_index // group_size
    offset = row_index % group_size * block_rows
    current = coefficients
    target = labels.astype(jnp.float32)
    residual = jnp.zeros((documents.shape[0], labels.shape[1]), jnp.float32)
    for iteration in range(ITERS):
        local_pred = jnp.dot(kernel, current, precision=highest, preferred_element_type=jnp.float32)
        predicted = lax.psum(local_pred, "col")
        residual = jax.nn.sigmoid(predicted) - target
        local_grad = lax.dot_general(
            kernel,
            residual,
            (((0,), (0,)), ((), ())),
            precision=highest,
            preferred_element_type=jnp.float32,
        )
        gradient = lax.psum(local_grad, "row")
        grad_block = lax.dynamic_slice_in_dim(gradient, offset, block_rows, 0)
        grad_block = broadcast(grad_block, "col", source)
        product_term = jnp.dot(
            inverse_tiles, grad_block, precision=highest, preferred_element_type=jnp.float32
        )
        current = current - step_size * lax.psum(product_term, "row")
    return (current, residual)


def solution(mesh):
    in_specs = (
        P("row", "col"),
        P("col", None),
        P("col", "row"),
        P("col", None),
        P("col", "row"),
        P("row", None),
    )
    out_specs = (P("col", None), P("row", None))
    return jax.shard_map(
        on_device, mesh=mesh, in_specs=in_specs, out_specs=out_specs, check_vma=False
    )
```

profile of v0, /device:TPU:0, one launch (start us, length us, event | category | flops | bytes accessed | tf_op | source)
XLA Modules:
  0.0 830.2 jit_solution(13493316278043722178)
XLA Ops:
  7.2 0.0 copy-start
  7.2 0.0 reduce-scatter.2.cloned.1.call-start
  7.2 1.0 copy-done
  8.2 4.6 fusion.11
  12.8 0.0 reduce-scatter.2.cloned.1.call-update
  12.8 0.0 all-gather.3.cloned.1.call-start
  12.9 50.5 %reduce-scatter.2.cloned.1.call-done = f32[192,768]{1,0:T(8,128)} async-done(((f32[768,768]{1,0:T(8,128)}), f32[192,768]{1,0:T(8,128)}) %reduce-scatter.2.cloned.1.call-update) | async-done | bytes 589840 | tf_op jit(solution)/shard_map/reduce_scatter | solution.py:19
  63.4 0.0 all-gather.3.cloned.1.call-update
  63.4 0.0 all-gather.5.cloned.1.call-start
  63.5 0.7 all-gather.5.cloned.1.call-update
  64.2 0.0 all-reduce.9.cloned.1.call-start
  64.2 50.2 %all-gather.3.cloned.1.call-done = f32[768,768]{1,0:T(8,128)} async-done(((f32[192,768]{1,0:T(8,128)}), f32[768,768]{1,0:T(8,128)}) %all-gather.3.cloned.1.call-update) | async-done | bytes 2359312 | tf_op jit(solution)/shard_map/all_gather | solution.py:25
  114.4 0.0 copy-start.5
  114.4 2.0 multiply_reduce_fusion.1
  116.4 70.6 %all-gather.5.cloned.1.call-done = f32[4096,768]{0,1:T(8,128)} async-done(((f32[4096,96]{0,1:T(8,128)}), f32[4096,768]{0,1:T(8,128)}) %all-gather.5.cloned.1.call-update) | async-done | bytes 12582928 | tf_op jit(solution)/shard_map/all_gather | solution.py:16
  187.1 0.0 copy-start.3
  187.1 5.9 multiply_reduce_fusion
  192.9 0.0 copy-done.5
  192.9 2.3 copy-done.3
  195.2 0.0 copy-start.4
  195.2 32.1 %multiply_exponential_fusion = f32[768,4096]{1,0:T(8,128)S(1)} fusion(f32[768,768]{1,0:T(8,128)S(1)} %copy-done.5, f32[4096,768]{0,1:T(8,128)S(1)} %copy-done.3, f32[4096]{0:T(1024)S(1)} %multiply_reduce_fusion, f32[768]{0:T(1024)S(1)} %multiply_reduce_fusion.1), kind=kOutput, calls=%fused_computation | convolution fusion | flops 29003612160 | bytes 27544576 | tf_op jit(solution)/shard_map/dot_general | solution.py:27
  227.4 0.0 copy-start.2
  227.4 4.5 copy-done.2
  231.9 0.0 copy-done.4
  231.9 10.6 %fusion.12 = f32[768,128]{1,0:T(8,128)} fusion(f32[768,4096]{1,0:T(8,128)S(1)} %multiply_exponential_fusion, f32[4096,128]{1,0:T(8,128)S(1)} %copy-done.4), kind=kOutput, calls=%fused_computation.22 | convolution fusion | flops 4831838208 | bytes 15073280 | tf_op jit(solution)/shard_map/dot_general | solution.py:47
  242.5 0.0 all-reduce.9.cloned.1.call-update
  242.6 0.0 all-reduce.11.cloned.1.call-start
  242.6 37.0 %all-reduce.9.cloned.1.call-done = f32[768,128]{1,0:T(8,128)} async-done(((f32[768,128]{1,0:T(8,128)}), f32[768,128]{1,0:T(8,128)}) %all-reduce.9.cloned.1.call-update) | async-done | bytes 393232 | tf_op jit(solution)/shard_map/psum | solution.py:48
  279.7 0.0 copy-done.6
  279.7 24.0 %fusion.1 = f32[4096,128]{1,0:T(8,128)} fusion(f32[768,4096]{1,0:T(8,128)} %copy-done.2, s32[768,128]{1,0:T(8,128)S(1)} %copy-done.6, f32[768,128]{1,0:T(8,128)} %all-reduce.9.cloned.1.call-done), kind=kOutput, calls=%fused_computation.11 | convolution fusion | flops 4832329728 | bytes 15466496 | tf_op jit(solution)/shard_map/dot_general | solution.py:50
  303.7 0.0 all-reduce.11.cloned.1.call-update
  303.7 0.0 all-reduce.13.cloned.1.call-start
  303.8 61.6 %all-reduce.11.cloned.1.call-done = f32[4096,128]{1,0:T(8,128)} async-done(((f32[4096,128]{1,0:T(8,128)}), f32[4096,128]{1,0:T(8,128)}) %all-reduce.11.cloned.1.call-update) | async-done | bytes 2097168 | tf_op jit(solution)/shard_map/psum | solution.py:57
  365.4 2.3 dynamic-slice_select_fusion.1
  367.6 0.0 all-reduce.13.cloned.1.call-update
  367.6 0.0 all-reduce.15.cloned.1.call-start
  367.7 51.5 %all-reduce.13.cloned.1.call-done = f32[2048,128]{1,0:T(8,128)} async-done(((f32[2048,128]{1,0:T(8,128)}), f32[2048,128]{1,0:T(8,128)}) %all-reduce.13.cloned.1.call-update) | async-done | bytes 1048592 | tf_op jit(solution)/shard_map/psum | solution.py:11
  419.1 42.4 %convolution_bitcast_fusion.1 = f32[4096,128]{0,1:T(8,128)} fusion(f32[2048,128]{1,0:T(8,128)} %all-reduce.13.cloned.1.call-done, f32[4096,2048]{1,0:T(8,128)} %param.10), kind=kOutput, calls=%fused_computation.3 | convolution fusion | flops 12884901888 | bytes 36700160 | tf_op jit(solution)/shard_map/dot_general | solution.py:60
  461.6 0.0 all-reduce.15.cloned.1.call-update
  461.6 0.0 all-reduce.17.cloned.1.call-start
  461.7 1.9 copy.8
  463.6 59.2 %all-reduce.15.cloned.1.call-done = f32[4096,128]{0,1:T(8,128)} async-done(((f32[4096,128]{0,1:T(8,128)}), f32[4096,128]{0,1:T(8,128)}) %all-reduce.15.cloned.1.call-update) | async-done | bytes 2097168 | tf_op jit(solution)/shard_map/psum | solution.py:63
  522.8 13.9 %fusion = f32[768,128]{1,0:T(8,128)} fusion(f32[768,4096]{1,0:T(8,128)} %copy-done.2, f32[4096,128]{0,1:T(8,128)S(1)} %copy.8, f32[4096,128]{0,1:T(8,128)} %all-reduce.15.cloned.1.call-done), kind=kOutput, calls=%fused_computation.9 | convolution fusion | flops 4832886784 | bytes 17170432 | tf_op jit(solution)/shard_map/dot_general | solution.py:47
  536.7 0.0 all-reduce.17.cloned.1.call-update
  536.7 0.0 all-reduce.19.cloned.1.call-start
  536.7 36.1 %all-reduce.17.cloned.1.call-done = f32[768,128]{1,0:T(8,128)} async-done(((f32[768,128]{1,0:T(8,128)}), f32[768,128]{1,0:T(8,128)}) %all-reduce.17.cloned.1.call-update) | async-done | bytes 393232 | tf_op jit(solution)/shard_map/psum | solution.py:48
  572.9 1.1 divide_subtract_fusion
  574.0 0.0 copy-start.7
  574.0 23.8 %fusion.13 = f32[4096,128]{1,0:T(8,128)} fusion(f32[768,4096]{1,0:T(8,128)} %copy-done.2, f32[768,128]{1,0:T(8,128)S(1)} %divide_subtract_fusion), kind=kOutput, calls=%fused_computation.23 | convolution fusion | flops 4831838208 | bytes 15073280 | tf_op jit(solution)/shard_map/dot_general | solution.py:50
  597.8 0.0 copy-done.7
  597.8 0.0 all-reduce.19.cloned.1.call-update
  597.8 0.0 all-reduce.21.cloned.1.call-start
  597.9 61.6 %all-reduce.19.cloned.1.call-done = f32[4096,128]{1,0:T(8,128)} async-done(((f32[4096,128]{1,0:T(8,128)}), f32[4096,128]{1,0:T(8,128)}) %all-reduce.19.cloned.1.call-update) | async-done | bytes 2097168 | tf_op jit(solution)/shard_map/psum | solution.py:57
  659.5 2.3 dynamic-slice_select_fusion
  661.8 0.0 all-reduce.21.cloned.1.call-update
  661.8 0.0 all-reduce.23.cloned.1.call-start
  661.9 51.4 %all-reduce.21.cloned.1.call-done = f32[2048,128]{1,0:T(8,128)} async-done(((f32[2048,128]{1,0:T(8,128)}), f32[2048,128]{1,0:T(8,128)}) %all-reduce.21.cloned.1.call-update) | async-done | bytes 1048592 | tf_op jit(solution)/shard_map/psum | solution.py:11
  713.3 42.0 %convolution_bitcast_fusion = f32[4096,128]{0,1:T(8,128)} fusion(f32[2048,128]{1,0:T(8,128)} %all-reduce.21.cloned.1.call-done, f32[4096,2048]{1,0:T(8,128)} %param.10), kind=kOutput, calls=%fused_computation.2 | convolution fusion | flops 12884901888 | bytes 36700160 | tf_op jit(solution)/shard_map/dot_general | solution.py:60
  755.3 0.0 all-reduce.23.cloned.1.call-update
  755.4 61.2 %all-reduce.23.cloned.1.call-done = f32[4096,128]{0,1:T(8,128)} async-done(((f32[4096,128]{0,1:T(8,128)}), f32[4096,128]{0,1:T(8,128)}) %all-reduce.23.cloned.1.call-update) | async-done | bytes 2097168 | tf_op jit(solution)/shard_map/psum | solution.py:63
  816.5 0.0 copy-start.1
  816.5 4.0 multiply_subtract_fusion
  820.6 2.9 copy.9
  823.4 0.0 copy-done.1
  (1 shorter events, 0.0 us)
Async XLA Ops:
  7.2 1.1 copy-start
  7.2 56.2 %reduce-scatter.2.cloned.1.call-start = ((), (), s32[]{:S(2)}) async-start(), calls=%async_computation.1 | async-start | bytes 2949120 | tf_op jit(solution)/shard_map/reduce_scatter | solution.py:19
  12.8 101.5 %all-gather.3.cloned.1.call-start = ((), (), s32[]{:S(2)}) async-start(), calls=%async_computation.2 | async-start | bytes 2949120 | tf_op jit(solution)/shard_map/all_gather | solution.py:25
  63.4 123.6 %all-gather.5.cloned.1.call-start = ((), (), s32[]{:S(2)}) async-start(), calls=%async_computation.3 | async-start | bytes 14155776 | tf_op jit(solution)/shard_map/all_gather | solution.py:16
  64.2 215.5 %all-reduce.9.cloned.1.call-start = ((), (), s32[]{:S(2)}) async-start(), calls=%async_computation.4 | async-start | bytes 786432 | tf_op jit(solution)/shard_map/psum | solution.py:48
  114.4 78.6 %copy-start.5 = (f32[768,768]{1,0:T(8,128)S(1)}, f32[768,768]{1,0:T(8,128)}, u32[]{:S(2)}) copy-start(f32[768,768]{1,0:T(8,128)} %all-gather.3.cloned.1.call-done) | copy-start | bytes 7077892
  187.1 8.2 copy-start.3
  195.2 36.7 %copy-start.4 = (f32[4096,128]{1,0:T(8,128)S(1)}, f32[4096,128]{1,0:T(8,128)}, u32[]{:S(2)}) copy-start(f32[4096,128]{1,0:T(8,128)} %param.9) | copy-start | bytes 6291460
  227.4 4.5 copy-start.2
  231.9 47.8 %copy-start.6 = (s32[768,128]{1,0:T(8,128)S(1)}, s32[768,128]{1,0:T(8,128)}, u32[]{:S(2)}) copy-start(s32[768,128]{1,0:T(8,128)} %param.11) | copy-start | bytes 1179652
  242.6 122.8 %all-reduce.11.cloned.1.call-start = ((), (), s32[]{:S(2)}) async-start(), calls=%async_computation.5 | async-start | bytes 4194304 | tf_op jit(solution)/shard_map/psum | solution.py:57
  303.7 115.4 %all-reduce.13.cloned.1.call-start = ((), (), s32[]{:S(2)}) async-start(), calls=%async_computation.6 | async-start | bytes 2097152 | tf_op jit(solution)/shard_map/psum | solution.py:11
  367.6 155.1 %all-reduce.15.cloned.1.call-start = ((), (), s32[]{:S(2)}) async-start(), calls=%async_computation.7 | async-start | bytes 4194304 | tf_op jit(solution)/shard_map/psum | solution.py:63
  461.6 111.3 %all-reduce.17.cloned.1.call-start = ((), (), s32[]{:S(2)}) async-start(), calls=%async_computation.8 | async-start | bytes 786432 | tf_op jit(solution)/shard_map/psum | solution.py:48
  536.7 122.8 %all-reduce.19.cloned.1.call-start = ((), (), s32[]{:S(2)}) async-start(), calls=%async_computation.9 | async-start | bytes 4194304 | tf_op jit(solution)/shard_map/psum | solution.py:57
  574.0 23.8 %copy-start.7 = (f32[768,128]{1,0:T(8,128)}, f32[768,128]{1,0:T(8,128)S(1)}, u32[]{:S(2)}) copy-start(f32[768,128]{1,0:T(8,128)S(1)} %divide_subtract_fusion) | copy-start | bytes 1179652
  597.8 115.5 %all-reduce.21.cloned.1.call-start = ((), (), s32[]{:S(2)}) async-start(), calls=%async_computation.10 | async-start | bytes 2097152 | tf_op jit(solution)/shard_map/psum | solution.py:11
  661.8 154.7 %all-reduce.23.cloned.1.call-start = ((), (), s32[]{:S(2)}) async-start(), calls=%async_computation.11 | async-start | bytes 4194304 | tf_op jit(solution)/shard_map/psum | solution.py:63
  816.5 6.9 copy-start.1
Sparse Core Ops, SparseCore 0:
  13.0 50.4 reduce-scatter.1
  65.0 49.3 all-gather.2
  116.3 70.7 all-gather.4
  242.7 36.9 all-reduce.8
  303.8 61.4 all-reduce.10
  368.2 50.9 all-reduce.12
  461.7 61.0 all-reduce.14
  536.8 36.0 all-reduce.16
  597.9 61.5 all-reduce.18
  662.3 50.9 all-reduce.20
  755.5 61.0 all-reduce.22
where the time goes:
time: 834 us; the launch traced here: 830 us
  waiting for transfers between devices  592 us (71%)
  matrix products  194 us (23%)
  other arithmetic  17.6 us (2%)
  between operations  14.2 us (2%)
  local copies, waits for them, and re-layouts  12.6 us (2%)
    psum x2, waiting for transfers between devices, on_device(): gradient = lax.psum(local_grad, 'row')  123 us
    psum x2, waiting for transfers between devices, on_device(): current = current - step_size * lax.psum(product_term, 'row')  120 us
    psum x2, waiting for transfers between devices, broadcast(): return lax.psum(block, axis)  103 us
    dot_general x2, matrix products, on_device(): jnp.dot(inverse_tiles, grad_block, precision=highest, preferred_element_t...  84.5 us
    psum x2, waiting for transfers between devices, on_device(): predicted = lax.psum(local_pred, 'col')  73.2 us
    all_gather x1, waiting for transfers between devices, on_device(): land_full = lax.all_gather(landmarks, 'row', axis=1, tiled=True)  70.6 us
    reduce_scatter x1, waiting for transfers between devices, on_device(): lax.psum_scatter(jnp.dot(documents, projection, precision=highest, prefer...  50.5 us
    all_gather x1, waiting for transfers between devices, on_device(): rows_in = lax.all_gather(proj_share, 'col', axis=0, tiled=True)  50.2 us
  transfers between devices with their start and end apart: 11, of which 11 were waited for; matrix products, arithmetic and copies ran while one was open for 0% of the time, Pallas kernels for 0%

commit v1 on v0

--- a/solution.py
+++ b/solution.py
@@ -13,7 +13,22 @@
 
 def on_device(documents, projection, landmarks, coefficients, inverse_tiles, labels):
     highest = lax.Precision.HIGHEST
-    land_full = lax.all_gather(landmarks, "row", axis=1, tiled=True)
+    ways, here, step = (lax.axis_size("row"), lax.axis_index("row"), landmarks.shape[1])
+    shape = [n * ways if d == 1 else n for d, n in enumerate(landmarks.shape)]
+    land_full = lax.dynamic_update_slice_in_dim(
+        jnp.zeros(shape, landmarks.dtype), landmarks, here * step, axis=1
+    )
+    going_up = going_down = landmarks
+    for far in range(1, ways // 2 + 1):
+        going_up = lax.ppermute(going_up, "row", [(d, (d + 1) % ways) for d in range(ways)])
+        land_full = lax.dynamic_update_slice_in_dim(
+            land_full, going_up, (here - far) % ways * step, axis=1
+        )
+        if 2 * far < ways:
+            going_down = lax.ppermute(going_down, "row", [(d, (d - 1) % ways) for d in range(ways)])
+            land_full = lax.dynamic_update_slice_in_dim(
+                land_full, going_down, (here + far) % ways * step, axis=1
+            )
     sq_land = jnp.sum(land_full * land_full, axis=1)
     feature_width = land_full.shape[1]
     proj_share = lax.psum_scatter(

time: 834 us -> 795 us (0.953)
  waiting for transfers between devices: 592 us -> 518 us
  local copies, waits for them, and re-layouts: 12.6 us -> 34 us
  starting transfers between devices: 0.45 us -> 10.4 us
    ppermute x0 -> x7, waiting for transfers between devices: none -> 93.2 us  [the longest x4 83.9 us: on_device(): lax.ppermute(going_up, 'row', [(d, (d + 1) % ways) for d in range(ways)])]
    all_gather x1 -> x0, waiting for transfers between devices: 70.6 us -> none  [on_device(): land_full = lax.all_gather(landmarks, 'row', axis=1, tiled=True)]
    reduce_scatter x1, waiting for transfers between devices: 50.5 us -> 0.01 us  [on_device(): lax.psum_scatter(jnp.dot(documents, projection, precision=highest, prefer...]
    all_gather x1, waiting for transfers between devices: 50.2 us -> 2.19 us  [on_device(): rows_in = lax.all_gather(proj_share, 'col', axis=0, tiled=True)]
    dynamic_update_slice x0 -> x8, local copies, waits for them, and re-layouts: none -> 17.3 us  [the longest x4 9.39 us: on_device(): lax.dynamic_update_slice_in_dim(land_full, going_up, (here - far) % ways...]
    ppermute x0 -> x7, starting transfers between devices: none -> 10 us  [the longest x3 8.48 us: on_device(): lax.ppermute(going_down, 'row', [(d, (d - 1) % ways) for d in range(ways)])]
  transfers between devices with their start and end apart: 11 -> 17, of which waited for: 11 -> 15; matrix products, arithmetic and copies ran while one was open for 0% -> 4% of each run, Pallas kernels for 0% -> 0%
where the time goes in v1:
time: 795 us; the launch traced here: 790 us
  waiting for transfers between devices  518 us (65%)
  matrix products  196 us (25%)
  local copies, waits for them, and re-layouts  34 us (4%)
  other arithmetic  17.4 us (2%)
  between operations  14.5 us (2%)
  starting transfers between devices  10.4 us (1%)
    psum x2, waiting for transfers between devices, on_device(): gradient = lax.psum(local_grad, 'row')  123 us
    psum x2, waiting for transfers between devices, on_device(): current = current - step_size * lax.psum(product_term, 'row')  120 us
    psum x2, waiting for transfers between devices, broadcast(): return lax.psum(block, axis)  103 us
    dot_general x2, matrix products, on_device(): jnp.dot(inverse_tiles, grad_block, precision=highest, preferred_element_t...  84.6 us
    ppermute x4, waiting for transfers between devices, on_device(): lax.ppermute(going_up, 'row', [(d, (d + 1) % ways) for d in range(ways)])  83.9 us
    psum x2, waiting for transfers between devices, on_device(): predicted = lax.psum(local_pred, 'col')  76.1 us
    dot_general x2, matrix products, on_device(): lax.dot_general(kernel, residual, (((0,), (0,)), ((), ())), precision=hig...  47.7 us
    dot_general x1, matrix products, on_device(): lax.dot_general(rows_in, land_full, (((1,), (1,)), ((), ())), precision=h...  34.6 us
  transfers between devices with their start and end apart: 17, of which 15 were waited for; matrix products, arithmetic and copies ran while one was open for 4% of the time, Pallas kernels for 0%

profile of v1, /device:TPU:0, one launch (start us, length us, event | category | flops | bytes accessed | tf_op | source)
XLA Modules:
  0.0 790.4 jit_solution(3696590498064333917)
XLA Ops:
  7.2 0.0 reduce-scatter.2.cloned.1.call-start
  7.2 1.0 copy-done
  8.2 4.5 fusion.11
  12.8 0.0 reduce-scatter.2.cloned.1.call-update
  12.8 0.0 all-gather.2.cloned.1.call-start
  12.9 0.5 collective-permute-start
  13.4 2.9 collective-permute-start.1
  16.4 32.3 %collective-permute-done = f32[4096,96]{0,1:T(8,128)S(1)} collective-permute-done((f32[4096,96]{0,1:T(8,128)S(1)}, f32[4096,96]{0,1:T(8,128)S(1)}, u32[]{:S(2)}, u32[]{:S(2)}) %collective-permute-start) | collective-permute-done | bytes 1572896 | tf_op jit(solution)/shard_map/ppermute | solution.py:23
  48.7 0.5 collective-permute-start.2
  49.2 0.9 collective-permute-done.1
  50.1 2.9 collective-permute-start.3
  53.0 30.6 %collective-permute-done.2 = f32[4096,96]{0,1:T(8,128)} collective-permute-done((f32[4096,96]{0,1:T(8,128)S(1)}, f32[4096,96]{0,1:T(8,128)}, u32[]{:S(2)}, u32[]{:S(2)}) %collective-permute-start.2) | collective-permute-done | bytes 1572896 | tf_op jit(solution)/shard_map/ppermute | solution.py:23
  83.6 6.1 broadcast_in_dim.2
  89.7 1.3 constant_dynamic-update-slice_fusion.7
  90.9 0.0 all-gather.2.cloned.1.call-update
  91.0 0.0 all-reduce.9.cloned.1.call-start
  91.0 2.7 constant_dynamic-update-slice_fusion.6
  93.7 2.6 collective-permute-start.5
  96.3 2.7 constant_dynamic-update-slice_fusion.5
  99.0 11.7 %collective-permute-done.4 = f32[4096,96]{0,1:T(8,128)} collective-permute-done((f32[4096,96]{0,1:T(8,128)}, f32[4096,96]{0,1:T(8,128)}, u32[]{:S(2)}, u32[]{:S(2)}) %collective-permute-start.4) | collective-permute-done | bytes 1572896 | tf_op jit(solution)/shard_map/ppermute | solution.py:23
  110.7 0.4 collective-permute-start.6
  111.2 2.7 constant_dynamic-update-slice_fusion.4
  113.8 2.7 constant_dynamic-update-slice_fusion.3
  116.5 2.8 constant_dynamic-update-slice_fusion.2
  119.3 8.4 %collective-permute-done.5 = f32[4096,96]{0,1:T(8,128)S(1)} collective-permute-done((f32[4096,96]{0,1:T(8,128)}, f32[4096,96]{0,1:T(8,128)S(1)}, u32[]{:S(2)}, u32[]{:S(2)}) %collective-permute-start.5) | collective-permute-done | bytes 1572896 | tf_op jit(solution)/shard_map/ppermute | solution.py:28
  127.7 1.3 constant_dynamic-update-slice_fusion.1
  129.0 9.3 %collective-permute-done.6 = f32[4096,96]{0,1:T(8,128)S(1)} collective-permute-done((f32[4096,96]{0,1:T(8,128)}, f32[4096,96]{0,1:T(8,128)S(1)}, u32[]{:S(2)}, u32[]{:S(2)}) %collective-permute-start.6) | collective-permute-done | bytes 1572896 | tf_op jit(solution)/shard_map/ppermute | solution.py:23
  138.2 1.2 constant_dynamic-update-slice_fusion
  139.5 5.7 multiply_reduce_fusion
  145.2 2.2 all-gather.2.cloned.1.call-done
  147.4 2.0 multiply_reduce_fusion.1
  149.4 0.3 copy-done.4
  149.8 34.6 %multiply_exponential_fusion = f32[768,4096]{1,0:T(8,128)S(1)} fusion(f32[768,768]{1,0:T(8,128)S(1)} %copy-done.4, f32[4096,768]{0,1:T(8,128)} %constant_dynamic-update-slice_fusion, f32[4096]{0:T(1024)S(1)} %multiply_reduce_fusion, f32[768]{0:T(1024)S(1)} %multiply_reduce_fusion.1), kind=kOutput, calls=%fused_computation | convolution fusion | flops 29003612160 | bytes 27544576 | tf_op jit(solution)/shard_map/dot_general | solution.py:42
  184.3 4.5 copy-done.2
  188.8 10.6 %fusion.12 = f32[768,128]{1,0:T(8,128)} fusion(f32[768,4096]{1,0:T(8,128)S(1)} %multiply_exponential_fusion, f32[4096,128]{1,0:T(8,128)S(1)} %copy-done.3), kind=kOutput, calls=%fused_computation.30 | convolution fusion | flops 4831838208 | bytes 15073280 | tf_op jit(solution)/shard_map/dot_general | solution.py:62
  199.5 0.0 all-reduce.9.cloned.1.call-update
  199.5 0.0 all-reduce.11.cloned.1.call-start
  199.6 40.0 %all-reduce.9.cloned.1.call-done = f32[768,128]{1,0:T(8,128)} async-done(((f32[768,128]{1,0:T(8,128)}), f32[768,128]{1,0:T(8,128)}) %all-reduce.9.cloned.1.call-update) | async-done | bytes 393232 | tf_op jit(solution)/shard_map/psum | solution.py:63
  239.5 23.9 %fusion.1 = f32[4096,128]{1,0:T(8,128)} fusion(f32[768,4096]{1,0:T(8,128)} %copy-done.2, s32[768,128]{1,0:T(8,128)S(1)} %copy-done.7, f32[768,128]{1,0:T(8,128)} %all-reduce.9.cloned.1.call-done), kind=kOutput, calls=%fused_computation.11 | convolution fusion | flops 4832329728 | bytes 15466496 | tf_op jit(solution)/shard_map/dot_general | solution.py:65
  263.4 0.0 all-reduce.13.cloned.1.call-start
  263.5 61.6 %all-reduce.11.cloned.1.call-done = f32[4096,128]{1,0:T(8,128)} async-done(((f32[4096,128]{1,0:T(8,128)}), f32[4096,128]{1,0:T(8,128)}) %all-reduce.11.cloned.1.call-update) | async-done | bytes 2097168 | tf_op jit(solution)/shard_map/psum | solution.py:72
  325.0 2.3 dynamic-slice_select_fusion.1
  327.3 0.0 all-reduce.15.cloned.1.call-start
  327.4 51.4 %all-reduce.13.cloned.1.call-done = f32[2048,128]{1,0:T(8,128)} async-done(((f32[2048,128]{1,0:T(8,128)}), f32[2048,128]{1,0:T(8,128)}) %all-reduce.13.cloned.1.call-update) | async-done | bytes 1048592 | tf_op jit(solution)/shard_map/psum | solution.py:11
  378.8 42.5 %convolution_bitcast_fusion.1 = f32[4096,128]{0,1:T(8,128)} fusion(f32[2048,128]{1,0:T(8,128)} %all-reduce.13.cloned.1.call-done, f32[4096,2048]{1,0:T(8,128)} %param.10), kind=kOutput, calls=%fused_computation.3 | convolution fusion | flops 12884901888 | bytes 36700160 | tf_op jit(solution)/shard_map/dot_general | solution.py:75
  421.3 0.0 all-reduce.15.cloned.1.call-update
  421.3 0.0 all-reduce.17.cloned.1.call-start
  421.4 1.9 copy.8
  423.3 59.2 %all-reduce.15.cloned.1.call-done = f32[4096,128]{0,1:T(8,128)} async-done(((f32[4096,128]{0,1:T(8,128)}), f32[4096,128]{0,1:T(8,128)}) %all-reduce.15.cloned.1.call-update) | async-done | bytes 2097168 | tf_op jit(solution)/shard_map/psum | solution.py:78
  482.5 13.9 %fusion = f32[768,128]{1,0:T(8,128)} fusion(f32[768,4096]{1,0:T(8,128)} %copy-done.2, f32[4096,128]{0,1:T(8,128)S(1)} %copy.8, f32[4096,128]{0,1:T(8,128)} %all-reduce.15.cloned.1.call-done), kind=kOutput, calls=%fused_computation.9 | convolution fusion | flops 4832886784 | bytes 17170432 | tf_op jit(solution)/shard_map/dot_general | solution.py:62
  496.4 0.0 all-reduce.19.cloned.1.call-start
  496.5 36.1 %all-reduce.17.cloned.1.call-done = f32[768,128]{1,0:T(8,128)} async-done(((f32[768,128]{1,0:T(8,128)}), f32[768,128]{1,0:T(8,128)}) %all-reduce.17.cloned.1.call-update) | async-done | bytes 393232 | tf_op jit(solution)/shard_map/psum | solution.py:63
  532.6 1.1 divide_subtract_fusion
  533.7 23.8 %fusion.13 = f32[4096,128]{1,0:T(8,128)} fusion(f32[768,4096]{1,0:T(8,128)} %copy-done.2, f32[768,128]{1,0:T(8,128)S(1)} %divide_subtract_fusion), kind=kOutput, calls=%fused_computation.31 | convolution fusion | flops 4831838208 | bytes 15073280 | tf_op jit(solution)/shard_map/dot_general | solution.py:65
  557.5 0.0 all-reduce.19.cloned.1.call-update
  557.5 0.0 all-reduce.21.cloned.1.call-start
  557.6 61.6 %all-reduce.19.cloned.1.call-done = f32[4096,128]{1,0:T(8,128)} async-done(((f32[4096,128]{1,0:T(8,128)}), f32[4096,128]{1,0:T(8,128)}) %all-reduce.19.cloned.1.call-update) | async-done | bytes 2097168 | tf_op jit(solution)/shard_map/psum | solution.py:72
  619.2 2.3 dynamic-slice_select_fusion
  621.5 0.0 all-reduce.23.cloned.1.call-start
  621.6 51.6 %all-reduce.21.cloned.1.call-done = f32[2048,128]{1,0:T(8,128)} async-done(((f32[2048,128]{1,0:T(8,128)}), f32[2048,128]{1,0:T(8,128)}) %all-reduce.21.cloned.1.call-update) | async-done | bytes 1048592 | tf_op jit(solution)/shard_map/psum | solution.py:11
  673.2 42.1 %convolution_bitcast_fusion = f32[4096,128]{0,1:T(8,128)} fusion(f32[2048,128]{1,0:T(8,128)} %all-reduce.21.cloned.1.call-done, f32[4096,2048]{1,0:T(8,128)} %param.10), kind=kOutput, calls=%fused_computation.2 | convolution fusion | flops 12884901888 | bytes 36700160 | tf_op jit(solution)/shard_map/dot_general | solution.py:75
  715.3 61.2 %all-reduce.23.cloned.1.call-done = f32[4096,128]{0,1:T(8,128)} async-done(((f32[4096,128]{0,1:T(8,128)}), f32[4096,128]{0,1:T(8,128)}) %all-reduce.23.cloned.1.call-update) | async-done | bytes 2097168 | tf_op jit(solution)/shard_map/psum | solution.py:78
  776.5 4.0 multiply_subtract_fusion
  780.5 2.9 copy.9
  (23 shorter events, 0.1 us)
Async XLA Ops:
  7.2 1.1 copy-start
  7.2 5.7 copy-start.5
  7.2 83.8 %reduce-scatter.2.cloned.1.call-start = ((), (), s32[]{:S(2)}) async-start(), calls=%async_computation.1 | async-start | bytes 2949120 | tf_op jit(solution)/shard_map/reduce_scatter | solution.py:34
  12.8 134.6 %all-gather.2.cloned.1.call-start = ((), (), s32[]{:S(2)}) async-start(), calls=%async_computation.2 | async-start | bytes 2949120 | tf_op jit(solution)/shard_map/all_gather | solution.py:40
  12.9 35.8 %collective-permute-start = (f32[4096,96]{0,1:T(8,128)S(1)}, f32[4096,96]{0,1:T(8,128)S(1)}, u32[]{:S(2)}, u32[]{:S(2)}) collective-permute-start(f32[4096,96]{0,1:T(8,128)S(1)} %copy-done.5), channel_id=1, source_target_pairs={{0,4},{4,8},{8,12},{12,16},{16,20},{20,24},{24,28},{28,0},{1,5},{5... | collective-permute-start | bytes 4718600 | tf_op jit(solution)/shard_map/ppermute | solution.py:23
  13.4 36.7 %collective-permute-start.1 = (f32[4096,96]{0,1:T(8,128)S(1)}, f32[4096,96]{0,1:T(8,128)}, u32[]{:S(2)}, u32[]{:S(2)}) collective-permute-start(f32[4096,96]{0,1:T(8,128)S(1)} %copy-done.5), channel_id=1, source_target_pairs={{0,28},{4,0},{8,4},{12,8},{16,12},{20,16},{24,20},{28,24},{1,29},{... | collective-permute-start | bytes 4718600 | tf_op jit(solution)/shard_map/ppermute | solution.py:28
  48.6 1.4 copy-start.6
  48.7 34.9 %collective-permute-start.2 = (f32[4096,96]{0,1:T(8,128)S(1)}, f32[4096,96]{0,1:T(8,128)}, u32[]{:S(2)}, u32[]{:S(2)}) collective-permute-start(f32[4096,96]{0,1:T(8,128)S(1)} %collective-permute-done), channel_id=1, source_target_pairs={{0,4},{4,8},{8,12},{12,16},{16,20},{20,24},{24,28},{28,0},{1,5},{5... | collective-permute-start | bytes 4718600 | tf_op jit(solution)/shard_map/ppermute | solution.py:23
  50.1 43.6 %collective-permute-start.3 = (f32[4096,96]{0,1:T(8,128)}, f32[4096,96]{0,1:T(8,128)}, u32[]{:S(2)}, u32[]{:S(2)}) collective-permute-start(f32[4096,96]{0,1:T(8,128)} %collective-permute-done.1), channel_id=1, source_target_pairs={{0,28},{4,0},{8,4},{12,8},{16,12},{20,16},{24,20},{28,24},{1,29},{... | collective-permute-start | bytes 4718600 | tf_op jit(solution)/shard_map/ppermute | solution.py:28
  83.6 27.1 %collective-permute-start.4 = (f32[4096,96]{0,1:T(8,128)}, f32[4096,96]{0,1:T(8,128)}, u32[]{:S(2)}, u32[]{:S(2)}) collective-permute-start(f32[4096,96]{0,1:T(8,128)} %collective-permute-done.2), channel_id=1, source_target_pairs={{0,4},{4,8},{8,12},{12,16},{16,20},{20,24},{24,28},{28,0},{1,5},{5... | collective-permute-start | bytes 4718600 | tf_op jit(solution)/shard_map/ppermute | solution.py:23
  91.0 148.5 %all-reduce.9.cloned.1.call-start = ((), (), s32[]{:S(2)}) async-start(), calls=%async_computation.3 | async-start | bytes 786432 | tf_op jit(solution)/shard_map/psum | solution.py:63
  93.7 34.0 %collective-permute-start.5 = (f32[4096,96]{0,1:T(8,128)}, f32[4096,96]{0,1:T(8,128)S(1)}, u32[]{:S(2)}, u32[]{:S(2)}) collective-permute-start(f32[4096,96]{0,1:T(8,128)} %collective-permute-done.3), channel_id=1, source_target_pairs={{0,28},{4,0},{8,4},{12,8},{16,12},{20,16},{24,20},{28,24},{1,29},{... | collective-permute-start | bytes 4718600 | tf_op jit(solution)/shard_map/ppermute | solution.py:28
  110.7 27.6 %collective-permute-start.6 = (f32[4096,96]{0,1:T(8,128)}, f32[4096,96]{0,1:T(8,128)S(1)}, u32[]{:S(2)}, u32[]{:S(2)}) collective-permute-start(f32[4096,96]{0,1:T(8,128)} %collective-permute-done.4), channel_id=1, source_target_pairs={{0,4},{4,8},{8,12},{12,16},{16,20},{20,24},{24,28},{28,0},{1,5},{5... | collective-permute-start | bytes 4718600 | tf_op jit(solution)/shard_map/ppermute | solution.py:23
  147.4 2.4 copy-start.4
  149.8 39.1 %copy-start.3 = (f32[4096,128]{1,0:T(8,128)S(1)}, f32[4096,128]{1,0:T(8,128)}, u32[]{:S(2)}) copy-start(f32[4096,128]{1,0:T(8,128)} %param.9) | copy-start | bytes 6291460
  184.3 4.5 copy-start.2
  188.8 50.7 %copy-start.7 = (s32[768,128]{1,0:T(8,128)S(1)}, s32[768,128]{1,0:T(8,128)}, u32[]{:S(2)}) copy-start(s32[768,128]{1,0:T(8,128)} %param.11) | copy-start | bytes 1179652
  199.5 125.5 %all-reduce.11.cloned.1.call-start = ((), (), s32[]{:S(2)}) async-start(), calls=%async_computation.4 | async-start | bytes 4194304 | tf_op jit(solution)/shard_map/psum | solution.py:72
  263.4 115.4 %all-reduce.13.cloned.1.call-start = ((), (), s32[]{:S(2)}) async-start(), calls=%async_computation.5 | async-start | bytes 2097152 | tf_op jit(solution)/shard_map/psum | solution.py:11
  327.3 155.2 %all-reduce.15.cloned.1.call-start = ((), (), s32[]{:S(2)}) async-start(), calls=%async_computation.6 | async-start | bytes 4194304 | tf_op jit(solution)/shard_map/psum | solution.py:78
  421.3 111.3 %all-reduce.17.cloned.1.call-start = ((), (), s32[]{:S(2)}) async-start(), calls=%async_computation.7 | async-start | bytes 786432 | tf_op jit(solution)/shard_map/psum | solution.py:63
  496.4 122.8 %all-reduce.19.cloned.1.call-start = ((), (), s32[]{:S(2)}) async-start(), calls=%async_computation.8 | async-start | bytes 4194304 | tf_op jit(solution)/shard_map/psum | solution.py:72
  533.7 23.8 %copy-start.8 = (f32[768,128]{1,0:T(8,128)}, f32[768,128]{1,0:T(8,128)S(1)}, u32[]{:S(2)}) copy-start(f32[768,128]{1,0:T(8,128)S(1)} %divide_subtract_fusion) | copy-start | bytes 1179652
  557.5 115.6 %all-reduce.21.cloned.1.call-start = ((), (), s32[]{:S(2)}) async-start(), calls=%async_computation.9 | async-start | bytes 2097152 | tf_op jit(solution)/shard_map/psum | solution.py:11
  621.5 154.9 %all-reduce.23.cloned.1.call-start = ((), (), s32[]{:S(2)}) async-start(), calls=%async_computation.10 | async-start | bytes 4194304 | tf_op jit(solution)/shard_map/psum | solution.py:78
  776.5 6.9 copy-start.1
Sparse Core Ops, SparseCore 0:
  12.9 50.4 reduce-scatter.1
  91.1 56.2 all-gather.1
  199.6 39.8 all-reduce.8
  263.5 61.4 all-reduce.10
  327.8 50.9 all-reduce.12
  421.4 61.0 all-reduce.14
  496.5 36.0 all-reduce.16
  557.7 61.5 all-reduce.18
  622.2 50.9 all-reduce.20
  715.4 61.0 all-reduce.22
